TPU v7x, 32 devices: a whole 2x2x4 slice. The times are simulated.
32 devices in a mesh: shard: 8 (over y, x, core), rep: 4 (over z).
Axes of the slice: x: 2, y: 2, z: 4, core: 2. Of those that a mesh axis runs over, the one named last changes fastest.
Arguments:
- inputs: bfloat16 [64, 256, 1024], P(('shard', 'rep')), may hold values from -6 to 6
- lengths: int32 [64], replicated, may hold values from 64 to 256, as said below
- dealing: int32 [64], replicated, may hold values from 0 to 63, as said below
- w_query: bfloat16 [1024, 1024], P('shard'), may hold values from -0.25 to 0.25
- w_key: bfloat16 [1024, 1024], P('shard'), may hold values from -0.25 to 0.25
- w_value: bfloat16 [1024, 1024], P('shard'), may hold values from -0.1875 to 0.1875
- w_out: bfloat16 [1024, 1024], P('shard'), may hold values from -0.5 to 0.5
- b_query: bfloat16 [1024], P('shard'), may hold values from -1.5 to 1.5
- b_value: bfloat16 [1024], P('shard'), may hold values from -1.5 to 1.5
- b_out: bfloat16 [1024], P('shard'), may hold values from -1.5 to 1.5
- ln1_gain: bfloat16 [1024], P('shard'), may hold values from 0.099609375 to 1.8984375
- ln1_bias: bfloat16 [1024], P('shard'), may hold values from -1.5 to 1.5
- w_up: bfloat16 [1024, 4096], P('shard'), may hold values from -0.1875 to 0.1875
- b_up: bfloat16 [4096], P('shard'), may hold values from -1.5 to 1.5
- w_down: bfloat16 [4096, 1024], P('shard'), may hold values from -0.09375 to 0.09375
- b_down: bfloat16 [1024], P('shard'), may hold values from -1.5 to 1.5
- ln2_gain: bfloat16 [1024], P('shard'), may hold values from 0.099609375 to 1.8984375
- ln2_bias: bfloat16 [1024], P('shard'), may hold values from -1.5 to 1.5
- cotangent: bfloat16 [64, 256, 1024], P(('shard', 'rep')), may hold values from -6 to 6
Outputs:
- layer_out: bfloat16 [64, 256, 1024], P(('shard', 'rep'))
- grad_input: bfloat16 [64, 256, 1024], P(('shard', 'rep'))
- grad_w_query: float32 [1024, 1024], P('shard')
- grad_w_key: float32 [1024, 1024], P('shard')
- grad_w_value: float32 [1024, 1024], P('shard')
- grad_w_out: float32 [1024, 1024], P('shard')
- grad_b_query: float32 [1024], P('shard')
- grad_b_value: float32 [1024], P('shard')
- grad_b_out: float32 [1024], P('shard')
- grad_ln1_gain: float32 [1024], P('shard')
- grad_ln1_bias: float32 [1024], P('shard')
- grad_w_up: float32 [1024, 4096], P('shard')
- grad_b_up: float32 [4096], P('shard')
- grad_w_down: float32 [4096, 1024], P('shard')
- grad_b_down: float32 [1024], P('shard')
- grad_ln2_gain: float32 [1024], P('shard')
- grad_ln2_bias: float32 [1024], P('shard')
Inputs may be any that keep to these rules, and one draw needn't show every extreme that they name: `lengths`: length of initial sequence; positions at or past it are padding. `dealing`: a permutation of the 64 sequences that maps each aligned block of 8 positions onto itself.
All inputs are finite; a program needn't handle non-finite values.
Results may differ from a plain program's by a relative error of at most 0.02.
Values may be sent and summed in bfloat16 or wider, within the bound.
No kernel may reach another device: no remote copies, remote signals or barrier semaphores. Data moves between devices by JAX's collectives and lax.ppermute only.
A program may use at most 192 MiB of HBM per device.

v0:
```python
import jax
import jax.numpy as jnp
from jax import lax
from jax.sharding import PartitionSpec as P

H = 16
HD = 64
EPS = 1e-05
NEG = -1e30
F32 = jnp.float32
BF16 = jnp.bfloat16


def matmul(left, right):
    return jnp.dot(left, right, preferred_element_type=F32)


def left_trans(left, right):
    return lax.dot_general(left, right, (((0,), (0,)), ((), ())), preferred_element_type=F32)


def right_trans(left, right):
    return lax.dot_general(left, right, (((1,), (1,)), ((), ())), preferred_element_type=F32)


def normalize(values, gain, shift):
    center = values - jnp.mean(values, -1, keepdims=True)
    inverse = lax.rsqrt(jnp.mean(center * center, -1, keepdims=True) + EPS)
    unit = center * inverse
    return (unit * gain + shift, unit, inverse)


def norm_back(grad, unit, inverse, gain):
    scaled = grad * gain
    return inverse * (
        scaled
        - jnp.mean(scaled, -1, keepdims=True)
        - unit * jnp.mean(scaled * unit, -1, keepdims=True)
    )


def gelu_both(pre):
    cumul = 0.5 * (1.0 + lax.erf(pre * 0.7071067811865476))
    density = jnp.exp(-0.5 * pre * pre) * 0.3989422804014327
    return (pre * cumul, cumul + pre * density)


def pick(pool, targets):
    return jnp.stack(
        [
            lax.dynamic_index_in_dim(pool, targets[i], 0, keepdims=False)
            for i in range(targets.shape[0])
        ]
    )


def local(
    inputs,
    lengths,
    dealing,
    w_query,
    w_key,
    w_value,
    w_out,
    b_query,
    b_value,
    b_out,
    ln1_gain,
    ln1_bias,
    w_up,
    b_up,
    w_down,
    b_down,
    ln2_gain,
    ln2_bias,
    cotangent,
):
    batches, rows, width = inputs.shape
    shards = lax.axis_size("shard")
    replicas = lax.axis_size("rep")
    group = batches * replicas
    shard_index = lax.axis_index("shard")
    rep_index = lax.axis_index("rep")
    anchor = shard_index * group
    slots = anchor + rep_index * batches + jnp.arange(batches, dtype=jnp.int32)
    seq_lengths = jnp.take(lengths, slots)
    local_dealing = lax.dynamic_slice_in_dim(dealing, anchor, group) - anchor
    sources = jnp.take(dealing, slots) - anchor
    places = jnp.arange(group, dtype=jnp.int32)
    wanted = jnp.sum(
        jnp.where(local_dealing[None, :] == (slots - anchor)[:, None], places[None, :], 0), 1
    )

    def gather(block):
        return lax.all_gather(block, "shard", axis=0, tiled=True)

    block = w_query.shape[0]
    wide = w_up.shape[1]
    small = (b_query, b_value, b_out, ln1_gain, ln1_bias, b_down, ln2_gain, ln2_bias, b_up)
    vec = jnp.concatenate(small)
    first = jnp.concatenate([w_query, w_key, w_value, w_out], 0)
    all_vec = lax.all_gather(vec, "shard", axis=0, tiled=True).reshape(shards, -1)
    all_first = gather(first).reshape(shards, 4, block, width)
    cuts = [0]
    for part in small:
        cuts.append(cuts[-1] + part.shape[0])
    (
        bias_query,
        bias_value,
        bias_out,
        gain_one,
        shift_one,
        bias_down,
        gain_two,
        shift_two,
        bias_up,
    ) = [all_vec[:, cuts[i] : cuts[i + 1]].reshape(-1).astype(F32) for i in range(len(small))]
    full_query, full_key, full_value, full_out = [
        all_first[:, i].reshape(width, width) for i in range(4)
    ]
    full_up = gather(w_up)
    full_down = gather(w_down)
    cot = pick(lax.all_gather(cotangent, "rep", axis=0, tiled=True), wanted)
    tokens = inputs.reshape(batches * rows, width)
    query = (matmul(tokens, full_query) + bias_query).astype(BF16)
    keyed = matmul(tokens, full_key).astype(BF16)
    value = (matmul(tokens, full_value) + bias_value).astype(BF16)
    heads = lambda a: a.reshape(batches, rows, H, HD).transpose(0, 2, 1, 3)
    flat = lambda a: a.transpose(0, 2, 1, 3).reshape(batches * rows, width)
    qh, kh, vh = (heads(query), heads(keyed), heads(value))
    allowed = (
        lax.broadcasted_iota(jnp.int32, (batches, 1, 1, rows), 3) < seq_lengths[:, None, None, None]
    )
    scale = HD ** (-0.5)
    scores = jnp.einsum("bhqd,bhkd->bhqk", qh, kh, preferred_element_type=F32) * scale
    scores = jnp.where(allowed, scores, NEG)
    raised = jnp.exp(scores - jnp.max(scores, -1, keepdims=True))
    probs = raised / jnp.sum(raised, -1, keepdims=True)
    probs_low = probs.astype(BF16)
    mixed_low = flat(
        jnp.einsum("bhqk,bhkd->bhqd", probs_low, vh, preferred_element_type=F32).astype(BF16)
    )
    hidden, unit_one, inverse_one = normalize(
        tokens.astype(F32) + matmul(mixed_low, full_out) + bias_out, gain_one, shift_one
    )
    hidden_low = hidden.astype(BF16)
    pre = matmul(hidden_low, full_up) + bias_up
    act, slope = gelu_both(pre)
    act_low = act.astype(BF16)
    summed = hidden + matmul(act_low, full_down) + bias_down
    normed, unit_two, inverse_two = normalize(summed, gain_two, shift_two)
    valid = (
        lax.broadcasted_iota(jnp.int32, (batches, rows, 1), 1) < seq_lengths[:, None, None]
    ).reshape(-1, 1)
    out = jnp.where(valid, normed, 0.0).astype(BF16).reshape(batches, rows, width)
    layer_out = pick(lax.all_gather(out, "rep", axis=0, tiled=True), sources)
    grad_out = jnp.where(valid, cot.reshape(-1, width).astype(F32), 0.0)
    grad_gain_two = jnp.sum(grad_out * unit_two, 0)
    grad_shift_two = jnp.sum(grad_out, 0)
    grad_sum = norm_back(grad_out, unit_two, inverse_two, gain_two)
    grad_bias_down = jnp.sum(grad_sum, 0)
    grad_sum_low = grad_sum.astype(BF16)

    def reduced(part):
        return lax.psum_scatter(part, "shard", scatter_dimension=0, tiled=True)

    def over_rep(part):
        return lax.psum(part, "rep").astype(F32)

    g_down = reduced(left_trans(act_low, grad_sum_low).astype(BF16))
    grad_pre = (right_trans(grad_sum_low, full_down) * slope).astype(BF16)
    grad_bias_up = jnp.sum(grad_pre.astype(F32), 0)
    g_up = reduced(left_trans(hidden_low, grad_pre).astype(BF16))
    grad_hidden = grad_sum + right_trans(grad_pre, full_up)
    grad_gain_one = jnp.sum(grad_hidden * unit_one, 0)
    grad_shift_one = jnp.sum(grad_hidden, 0)
    grad_resid = norm_back(grad_hidden, unit_one, inverse_one, gain_one)
    grad_bias_out = jnp.sum(grad_resid, 0)
    grad_resid_low = grad_resid.astype(BF16)
    grad_w_out = left_trans(mixed_low, grad_resid_low).astype(BF16)
    grad_mixed = heads(right_trans(grad_resid_low, full_out).astype(BF16))
    grad_probs = jnp.einsum("bhqd,bhkd->bhqk", grad_mixed, vh, preferred_element_type=F32)
    inner = jnp.sum(probs * grad_probs, -1, keepdims=True)
    grad_scores = (probs * (grad_probs - inner) * scale).astype(BF16)
    query_low = flat(
        jnp.einsum("bhqk,bhkd->bhqd", grad_scores, kh, preferred_element_type=F32).astype(BF16)
    )
    key_low = flat(
        jnp.einsum("bhqk,bhqd->bhkd", grad_scores, qh, preferred_element_type=F32).astype(BF16)
    )
    value_low = flat(
        jnp.einsum("bhqk,bhqd->bhkd", probs_low, grad_mixed, preferred_element_type=F32).astype(
            BF16
        )
    )
    grad_bias_query = jnp.sum(query_low.astype(F32), 0)
    grad_bias_value = jnp.sum(value_low.astype(F32), 0)
    blocks = [
        part.reshape(shards, block, width)
        for part in (
            left_trans(tokens, query_low).astype(BF16),
            left_trans(tokens, key_low).astype(BF16),
            left_trans(tokens, value_low).astype(BF16),
            grad_w_out,
        )
    ]
    g_first = reduced(jnp.concatenate(blocks, 1).reshape(shards * 4 * block, width))
    grad_tokens = (
        grad_resid
        + right_trans(query_low, full_query)
        + right_trans(key_low, full_key)
        + right_trans(value_low, full_value)
    )
    grad_input = grad_tokens.astype(BF16).reshape(batches, rows, width)
    vec_terms = (
        grad_bias_query,
        grad_bias_value,
        grad_bias_out,
        grad_gain_one,
        grad_shift_one,
        grad_bias_down,
        grad_gain_two,
        grad_shift_two,
        grad_bias_up,
    )
    g_vec = jnp.concatenate([part.reshape(shards, -1) for part in vec_terms], 1)
    g_vec = lax.psum(g_vec, ("shard", "rep"))
    g_vec = lax.dynamic_index_in_dim(g_vec, shard_index, 0, keepdims=False)
    g_bquery, g_bvalue, g_bout, g_gain_one, g_shift_one, g_bdown, g_gain_two, g_shift_two, g_bup = [
        g_vec[cuts[i] : cuts[i + 1]] for i in range(len(small))
    ]
    g_down = over_rep(g_down)
    g_up = over_rep(g_up)
    g_first = over_rep(g_first).reshape(4, block, width)
    return (
        layer_out,
        grad_input,
        g_first[0],
        g_first[1],
        g_first[2],
        g_first[3],
        g_bquery,
        g_bvalue,
        g_bout,
        g_gain_one,
        g_shift_one,
        g_up,
        g_bup,
        g_down,
        g_bdown,
        g_gain_two,
        g_shift_two,
    )


def solution(mesh):
    seqs = P(("shard", "rep"), None, None)
    mat = P("shard", None)
    vec = P("shard")
    in_specs = (
        seqs,
        P(),
        P(),
        mat,
        mat,
        mat,
        mat,
        vec,
        vec,
        vec,
        vec,
        vec,
        mat,
        vec,
        mat,
        vec,
        vec,
        vec,
        seqs,
    )
    out_specs = (
        seqs,
        seqs,
        mat,
        mat,
        mat,
        mat,
        vec,
        vec,
        vec,
        vec,
        vec,
        mat,
        vec,
        mat,
        vec,
        vec,
        vec,
    )
    return jax.shard_map(local, mesh=mesh, in_specs=in_specs, out_specs=out_specs, check_vma=False)
```

profile of v0, /device:TPU:0, one launch (start us, length us, event | category | flops | bytes accessed | tf_op | source)
XLA Modules:
  0.0 790.4 jit_solution(13564791712874749416)
XLA Ops:
  8.0 2.2 pad_maximum_fusion.1
  18.1 10.6 %all-gather = bf16[8,1,1536]{2,1,0:T(2,128)(2,1)S(1)} all-gather(bf16[1,1,1536]{2,1,0:T(2,128)(2,1)S(1)} %reshape.383), channel_id=1, replica_groups=mesh['shard'=8,'rep'=4] {'shard'}, dimensions={0}, use_global_device_ids=true | all-gather | bytes 27648 | tf_op jit(solution)/shard_map/all_gather | solution.py:102
  30.9 62.3 %all-gather.15.cloned.1.call-done = bf16[8,256,1024]{2,1,0:T(8,128)(2,1)} async-done(((bf16[2,256,1024]{2,1,0:T(8,128)(2,1)}), bf16[8,256,1024]{2,1,0:T(8,128)(2,1)}) %all-gather.15.cloned.1.call-update) | async-done | bytes 4194320 | tf_op jit(solution)/shard_map/all_gather | solution.py:123
  95.5 53.0 %all-gather.7.cloned.1.call-done = bf16[4096,1024]{1,0:T(8,128)(2,1)} async-done(((bf16[512,1024]{1,0:T(8,128)(2,1)}), bf16[4096,1024]{1,0:T(8,128)(2,1)}) %all-gather.7.cloned.1.call-update) | async-done | bytes 8388624 | tf_op jit(solution)/shard_map/all_gather | solution.py:95
  148.5 5.9 fusion.97
  154.4 1.3 copy-done.6
  155.8 1.3 fusion.54
  157.4 4.7 fusion.43
  162.1 1.3 reshape.332
  163.5 4.5 fusion.53
  168.0 2.1 reshape.331
  170.1 2.5 fusion.59
  172.6 3.5 fusion.101
  177.0 3.3 copy-done.41
  182.2 1.4 fusion.102
  183.9 20.9 %all-gather.9.cloned.1.call-done = bf16[1024,4096]{1,0:T(8,128)(2,1)} async-done(((bf16[128,4096]{1,0:T(8,128)(2,1)}), bf16[1024,4096]{1,0:T(8,128)(2,1)}) %all-gather.9.cloned.1.call-update) | async-done | bytes 8388624 | tf_op jit(solution)/shard_map/all_gather | solution.py:95
  204.8 10.9 %multiply_convert_fusion.1 = (bf16[512,4096]{1,0:T(8,128)(2,1)}, f32[512,4096]{1,0:T(8,128)}) fusion(f32[4096]{0:T(1024)S(1)} %bitcast.241, bf16[1024,4096]{1,0:T(8,128)(2,1)} %all-gather.9.cloned.1.call-done, f32[512,1024]{1,0:T(8,128)S(1)} %get-tuple-element.69, f32[1024]{0:T(1024)S(1)} %get-tuple-element.57, f32[1024]{0:T(1024)S(1)} %get-tuple-element.58, ...), kind=kOutput, calls=%fused_computation.16 | convolution fusion | flops 4310171648 | bytes 23097344 | tf_op jit(solution)/shard_map/dot_general | solution.py:15
  215.8 45.2 %all-gather.11.cloned.1.call-done = bf16[4096,1024]{1,0:T(8,128)(2,1)} async-done(((bf16[512,1024]{1,0:T(8,128)(2,1)}), bf16[4096,1024]{1,0:T(8,128)(2,1)}) %all-gather.11.cloned.1.call-update) | async-done | bytes 8388624 | tf_op jit(solution)/shard_map/all_gather | solution.py:95
  261.0 8.5 %fusion.103 = (f32[512]{0:T(512)S(1)}, f32[512,1024]{1,0:T(8,128)S(1)}) fusion(f32[1024]{0:T(1024)S(1)} %get-tuple-element.56, bf16[512,4096]{1,0:T(8,128)(2,1)} %get-tuple-element.70, bf16[4096,1024]{1,0:T(8,128)(2,1)} %all-gather.11.cloned.1.call-done, f32[1024]{0:T(1024)S(1)} %get-tuple-element.57, f32[1024]{0:T(1024)S(1)} %get-tuple-element.58, ...), kind=kOutput, calls=%fused_computation.175 | convolution fusion | flops 4298636800 | bytes 16795648 | tf_op jit(solution)/shard_map/dot_general | solution.py:15
  270.7 2.2 fusion.95
  273.0 11.9 %convert_reduce_fusion = (f32[4096]{0:T(1024)S(1)}, bf16[512,4096]{1,0:T(8,128)(2,1)S(1)}) fusion(f32[512,4096]{1,0:T(8,128)} %get-tuple-element.71, f32[4096]{0:T(1024)S(1)} %bitcast.242, bf16[4096,1024]{1,0:T(8,128)(2,1)} %all-gather.11.cloned.1.call-done, f32[512,1024]{1,0:T(8,128)S(1)} %get-tuple-element.30), kind=kOutput, calls=%fused_computation.12 | convolution fusion | flops 4322750464 | bytes 23101440 | tf_op jit(solution)/shard_map/dot_general | solution.py:23
  285.0 5.2 multiply_reduce_fusion.2
  290.9 1.3 copy-done.3
  292.3 2.3 convolution_convert_fusion.6
  294.5 2.4 copy.77
  296.9 2.1 reshape.336
  299.0 5.8 fusion.55
  304.8 13.5 %fusion.44 = bf16[2,256,16,64]{1,3,2,0:T(8,128)(2,1)} fusion(f32[2,16,256,256]{2,3,1,0:T(8,128)} %fusion.55, bf16[2,256,16,64]{1,0,3,2:T(2,128)(2,1)} %reshape.331, f32[2,16,256,256]{2,3,1,0:T(8,128)} %copy-done.41, f32[2,16,256]{2,1,0:T(8,128)S(1)} %get-tuple-element.66), kind=kOutput, calls=%fused_computation.72 | convolution fusion | flops 283648256 | bytes 18907136 | tf_op jit(solution)/shard_map/bhqk,bhqd->bhkd/dot_general | solution.py:189
  318.3 13.3 %convert_reduce_fusion.2 = (f32[16,64]{1,0:T(8,128)S(1)}, bf16[2,256,16,64]{1,3,2,0:T(8,128)(2,1)}) fusion(f32[2,16,256,256]{2,3,1,0:T(8,128)} %fusion.55, f32[2,16,256,256]{2,3,1,0:T(8,128)} %copy-done.41, f32[2,16,256]{2,1,0:T(8,128)S(1)} %get-tuple-element.66, bf16[2,256,16,64]{1,0,3,2:T(2,128)(2,1)S(1)} %copy-done.11), kind=kOutput, calls=%fused_computation.33 | convolution fusion | flops 284695808 | bytes 18911232 | tf_op jit(solution)/shard_map/bhqk,bhkd->bhqd/dot_general | solution.py:186
  331.6 5.2 convert_reduce_fusion.1
  342.4 1.3 convolution_convert_fusion.3
  343.7 1.3 convolution_convert_fusion.4
  345.1 1.3 convolution_convert_fusion.5
  346.4 3.7 pad_maximum_fusion
  350.1 9.8 %convolution_convert_fusion.1 = bf16[1024,4096]{1,0:T(8,128)(2,1)} fusion(bf16[512,4096]{1,0:T(8,128)(2,1)} %copy-done.42, f32[512,1024]{1,0:T(8,128)S(1)} %get-tuple-element.69, f32[1024]{0:T(1024)S(1)} %get-tuple-element.57, f32[1024]{0:T(1024)S(1)} %get-tuple-element.58, f32[512]{0:T(512)S(1)} %add_rsqrt_fusion.1, f32[512]{0:T(512)S(1)} %broadcast_multiply_fusion.4), kind=kOutput, calls=%fused_computation.21 | convolution fusion | flops 4301783040 | bytes 14692352 | tf_op jit(solution)/shard_map/dot_general | solution.py:19
  360.0 2.0 copy-done.17
  362.0 9.9 %convolution_convert_fusion = bf16[4096,1024]{1,0:T(8,128)(2,1)} fusion(bf16[512,4096]{1,0:T(8,128)(2,1)} %get-tuple-element.70, f32[512,1024]{1,0:T(8,128)S(1)} %copy-done.17), kind=kOutput, calls=%fused_computation.20 | convolution fusion | flops 4299685888 | bytes 14680064 | tf_op jit(solution)/shard_map/dot_general | solution.py:19
  377.3 44.2 %reduce-scatter.4.cloned.1.call-done = bf16[512,1024]{1,0:T(8,128)(2,1)} async-done(((bf16[4096,1024]{1,0:T(8,128)(2,1)}), bf16[512,1024]{1,0:T(8,128)(2,1)}) %reduce-scatter.4.cloned.1.call-update) | async-done | bytes 1048592 | tf_op jit(solution)/shard_map/reduce_scatter | solution.py:165
  421.6 75.0 %reduce-scatter.6.cloned.1.call-done = bf16[128,4096]{1,0:T(8,128)(2,1)} async-done(((bf16[1024,4096]{1,0:T(8,128)(2,1)}), bf16[128,4096]{1,0:T(8,128)(2,1)}) %reduce-scatter.6.cloned.1.call-update) | async-done | bytes 1048592 | tf_op jit(solution)/shard_map/reduce_scatter | solution.py:165
  496.6 74.7 %reduce-scatter.8.cloned.1.call-done = bf16[512,1024]{1,0:T(8,128)(2,1)} async-done(((bf16[4096,1024]{1,0:T(8,128)(2,1)}), bf16[512,1024]{1,0:T(8,128)(2,1)}) %reduce-scatter.8.cloned.1.call-update) | async-done | bytes 1048592 | tf_op jit(solution)/shard_map/reduce_scatter | solution.py:165
  571.4 43.1 %psum.29 = f32[8,1536]{1,0:T(8,128)S(1)} all-reduce(f32[8,1536]{1,0:T(8,128)S(1)} %constant_dynamic-update-slice_fusion), channel_id=1, replica_groups=mesh['shard'=8,'rep'=4] {'shard','rep'}, use_global_device_ids=true, to_apply=%region_23.25 | all-reduce | flops 12288 | bytes 98304 | tf_op jit(solution)/shard_map/psum | solution.py:227
  615.9 2.7 fusion.107
  620.9 2.3 add_convert_fusion
  623.2 31.6 %all-gather.13.cloned.1.call-done = bf16[8,256,1024]{2,1,0:T(8,128)(2,1)} async-done(((bf16[2,256,1024]{2,1,0:T(8,128)(2,1)}), bf16[8,256,1024]{2,1,0:T(8,128)(2,1)}) %all-gather.13.cloned.1.call-update) | async-done | bytes 4194320 | tf_op jit(solution)/shard_map/all_gather | solution.py:156
  657.2 120.7 %all-reduce.3.cloned.1.call-done = (bf16[512,1024]{1,0:T(8,128)(2,1)}, bf16[128,4096]{1,0:T(8,128)(2,1)}, bf16[512,1024]{1,0:T(8,128)(2,1)}) async-done(((bf16[512,1024]{1,0:T(8,128)(2,1)}, bf16[128,4096]{1,0:T(8,128)(2,1)}, bf16[512,1024]{1,0:T(8,128)(2,1)}), (bf16[512,1024]{1,0:T(8,128)(2,1)}, bf16[128,4096]{1,0:T(8,128)(2,1)}, bf16[512,1024]{1,0:T(8,128)(2,1)})) %all-reduce.3.cloned.1.call-update) | async-done | bytes 3145744 | tf_op jit(solution)/shard_map/psum | solution.py:168
  777.8 2.7 fusion.98
  780.5 1.5 convert_element_type.284
  782.0 1.6 convert_element_type.286
  (175 shorter events, 27.3 us)
Async XLA Ops:
  7.2 21.6 %copy-start = (s32[64]{0:T(128)S(1)}, s32[64]{0:T(128)}, u32[]{:S(2)}) copy-start(s32[64]{0:T(128)} %param.22) | copy-start | bytes 772
  7.2 86.0 %all-gather.15.cloned.1.call-start = ((), (), s32[]{:S(2)}) async-start(), calls=%async_computation.7 | async-start | bytes 5242880 | tf_op jit(solution)/shard_map/all_gather | solution.py:123
  7.9 140.6 %all-gather.7.cloned.1.call-start = ((), (), s32[]{:S(2)}) async-start(), calls=%async_computation.3 | async-start | bytes 9437184 | tf_op jit(solution)/shard_map/all_gather | solution.py:95
  10.2 6.1 copy-start.33
  10.2 6.4 copy-start.34
  10.2 6.6 copy-start.35
  10.2 6.8 copy-start.36
  10.2 7.0 copy-start.37
  10.3 7.2 copy-start.38
  10.3 7.4 copy-start.39
  10.3 7.6 copy-start.40
  10.3 7.8 copy-start.32
  10.3 194.5 %all-gather.9.cloned.1.call-start = ((), (), s32[]{:S(2)}) async-start(), calls=%async_computation.4 | async-start | bytes 9437184 | tf_op jit(solution)/shard_map/all_gather | solution.py:95
  11.1 249.9 %all-gather.11.cloned.1.call-start = ((), (), s32[]{:S(2)}) async-start(), calls=%async_computation.5 | async-start | bytes 9437184 | tf_op jit(solution)/shard_map/all_gather | solution.py:95
  11.6 409.9 %reduce-scatter.4.cloned.1.call-start = ((), (), s32[]{:S(2)}) async-start(), calls=%async_computation.8 | async-start | bytes 9437184 | tf_op jit(solution)/shard_map/reduce_scatter | solution.py:165
  148.5 7.3 copy-start.27
  157.4 18.8 %copy-start.12 = (bf16[2,256,16,64]{1,0,3,2:T(2,128)(2,1)}, bf16[2,256,16,64]{1,0,3,2:T(2,128)(2,1)S(1)}, u32[]{:S(2)}) copy-start(bf16[2,256,16,64]{1,0,3,2:T(2,128)(2,1)S(1)} %reshape.333) | copy-start | bytes 3145732
  163.5 6.7 copy-start.10
  176.1 4.2 copy-start.41
  180.3 1.6 copy-start.8
  180.3 1.9 copy-start.28
  181.6 1.9 copy-start.14
  270.7 14.2 %slice-start = ((s8[8388608]{0:T(1024)(128)(4,1)}), s8[4194304]{0:T(1024)(128)(4,1)S(1)}, s32[]{:S(2)}) async-start(s8[8388608]{0:T(1024)(128)(4,1)} %bitcast.245), calls=%async_computation.12 | async-start | bytes 8388608
  273.0 12.0 %copy-start.16 = (f32[512,1024]{1,0:T(8,128)}, f32[512,1024]{1,0:T(8,128)S(1)}, u32[]{:S(2)}) copy-start(f32[512,1024]{1,0:T(8,128)S(1)} %get-tuple-element.30) | copy-start | bytes 6291460
  273.0 12.0 %slice-start.1 = ((s8[8388608]{0:T(1024)(128)(4,1)}), s8[4194304]{0:T(1024)(128)(4,1)S(1)}, s32[]{:S(2)}) async-start(s8[8388608]{0:T(1024)(128)(4,1)} %bitcast.245), calls=%async_computation.13 | async-start | bytes 8388608
  284.9 5.3 copy-start.42
  290.2 2.1 copy-start.9
  294.5 4.5 copy-start.13
  304.8 13.5 %copy-start.11 = (bf16[2,256,16,64]{1,0,3,2:T(2,128)(2,1)S(1)}, bf16[2,256,16,64]{1,0,3,2:T(2,128)(2,1)}, u32[]{:S(2)}) copy-start(bf16[2,256,16,64]{1,0,3,2:T(2,128)(2,1)} %copy-done.10) | copy-start | bytes 3145732
  331.5 5.3 copy-start.4
  331.6 5.3 copy-start.15
  339.4 4.3 copy-start.22
  340.8 4.2 copy-start.23
  340.8 1.6 copy-start.29
  350.1 146.5 %reduce-scatter.6.cloned.1.call-start = ((), (), s32[]{:S(2)}) async-start(), calls=%async_computation.9 | async-start | bytes 9437184 | tf_op jit(solution)/shard_map/reduce_scatter | solution.py:165
  359.9 2.0 copy-start.17
  360.0 211.4 %reduce-scatter.8.cloned.1.call-start = ((), (), s32[]{:S(2)}) async-start(), calls=%async_computation.10 | async-start | bytes 9437184 | tf_op jit(solution)/shard_map/reduce_scatter | solution.py:165
  371.9 282.9 %all-gather.13.cloned.1.call-start = ((), (), s32[]{:S(2)}) async-start(), calls=%async_computation.6 | async-start | bytes 5242880 | tf_op jit(solution)/shard_map/all_gather | solution.py:156
  371.9 199.5 %copy-start.30 = (f32[1024]{0:T(1024)S(1)}, f32[1024]{0:T(1024)}, u32[]{:S(2)}) copy-start(f32[1024]{0:T(1024)} %get-tuple-element.24) | copy-start | bytes 12292
  371.9 243.9 %copy-start.19 = (bf16[8,1,128,1024]{3,2,1,0:T(8,128)(2,1)S(1)}, bf16[8,1,128,1024]{3,2,1,0:T(8,128)(2,1)}, u32[]{:S(2)}) copy-start(bf16[8,1,128,1024]{3,2,1,0:T(8,128)(2,1)} %get-tuple-element.35) | copy-start | bytes 6291460
  372.6 405.2 %all-reduce.3.cloned.1.call-start = ((), (), s32[]{:S(2)}) async-start(), calls=%async_computation.11 | async-start | bytes 6291456 | tf_op jit(solution)/shard_map/psum | solution.py:168
  615.9 2.7 copy-start.18
  615.9 2.7 copy-start.24
  618.6 1.6 copy-start.5
  618.6 2.2 copy-start.7
  777.8 2.7 copy-start.21
  780.5 1.5 copy-start.20
  780.5 3.1 copy-start.1
  (6 other events, 7.7 us)
Sparse Core Ops, SparseCore 0:
  9.6 83.5 all-gather.14
  95.6 52.8 all-gather.6
  150.4 54.3 all-gather.8
  206.6 54.3 all-gather.10
  350.2 71.2 reduce-scatter.3
  425.3 71.2 reduce-scatter.5
  500.0 71.2 reduce-scatter.7
  573.0 81.7 all-gather.12
  657.6 120.2 all-reduce.2
where the time goes:
time: 794 us; the launch traced here: 790 us
  waiting for transfers between devices  530 us (67%)
  matrix products  123 us (15%)
  blocking collectives  53.8 us (7%)
  local copies, waits for them, and re-layouts  40.2 us (5%)
  between operations  22.6 us (3%)
  other arithmetic  20 us (3%)
    reduce_scatter x3, waiting for transfers between devices, reduced(): return lax.psum_scatter(part, 'shard', scatter_dimension=0, tiled=True)  194 us
    psum x1, waiting for transfers between devices, over_rep(): return lax.psum(part, 'rep').astype(F32)  121 us
    all_gather x3, waiting for transfers between devices, gather(): return lax.all_gather(block, 'shard', axis=0, tiled=True)  119 us
    all_gather x1, waiting for transfers between devices, local(): cot = pick(lax.all_gather(cotangent, 'rep', axis=0, tiled=True), wanted)  62.3 us
    psum x1, blocking collectives, local(): g_vec = lax.psum(g_vec, ('shard', 'rep'))  43.1 us
    all_gather x1, waiting for transfers between devices, local(): layer_out = pick(lax.all_gather(out, 'rep', axis=0, tiled=True), sources)  31.6 us
    dot_general x6, matrix products, matmul(): return jnp.dot(left, right, preferred_element_type=F32)  31.3 us
    dot_general x6, matrix products, right_trans(): lax.dot_general(left, right, (((1,), (1,)), ((), ())), preferred_element_...  25.8 us
  transfers between devices with their start and end apart: 9, of which 9 were waited for; matrix products, arithmetic and copies ran while one was open for 10% of the time, Pallas kernels for 0%

commit v1 on v0

--- a/solution.py
+++ b/solution.py
@@ -9,6 +9,12 @@
 NEG = -1e30
 F32 = jnp.float32
 BF16 = jnp.bfloat16
+
+
+def summed_here(array, axis):
+    parts = lax.all_gather(array, axis, axis=0, tiled=False)
+    total = parts.sum(axis=0)
+    return total
 
 
 def matmul(left, right):
@@ -165,7 +171,7 @@
         return lax.psum_scatter(part, "shard", scatter_dimension=0, tiled=True)
 
     def over_rep(part):
-        return lax.psum(part, "rep").astype(F32)
+        return summed_here(part, "rep").astype(F32)
 
     g_down = reduced(left_trans(act_low, grad_sum_low).astype(BF16))
     grad_pre = (right_trans(grad_sum_low, full_down) * slope).astype(BF16)

time: 794 us -> 913 us (1.15)
  waiting for transfers between devices: 530 us -> 640 us
  other arithmetic: 20 us -> 29.7 us
    all_gather x0 -> x3, waiting for transfers between devices: none -> 231 us  [summed_here(): parts = lax.all_gather(array, axis, axis=0, tiled=False)]
    psum x1 -> x0, waiting for transfers between devices: 121 us -> none  [over_rep(): return lax.psum(part, 'rep').astype(F32)]
    reduce_sum x0 -> x3, other arithmetic: none -> 9.72 us  [summed_here(): total = parts.sum(axis=0)]
  transfers between devices with their start and end apart: 9 -> 11, of which waited for: 9 -> 11; matrix products, arithmetic and copies ran while one was open for 10% -> 10% of each run, Pallas kernels for 0% -> 0%
where the time goes in v1:
time: 913 us; the launch traced here: 909 us
  waiting for transfers between devices  640 us (70%)
  matrix products  123 us (13%)
  blocking collectives  54.2 us (6%)
  local copies, waits for them, and re-layouts  38.8 us (4%)
  other arithmetic  29.7 us (3%)
  between operations  22.6 us (2%)
    all_gather x3, waiting for transfers between devices, summed_here(): parts = lax.all_gather(array, axis, axis=0, tiled=False)  231 us
    reduce_scatter x3, waiting for transfers between devices, reduced(): return lax.psum_scatter(part, 'shard', scatter_dimension=0, tiled=True)  198 us
    all_gather x3, waiting for transfers between devices, gather(): return lax.all_gather(block, 'shard', axis=0, tiled=True)  119 us
    all_gather x1, waiting for transfers between devices, local(): cot = pick(lax.all_gather(cotangent, 'rep', axis=0, tiled=True), wanted)  62.3 us
    psum x1, blocking collectives, local(): g_vec = lax.psum(g_vec, ('shard', 'rep'))  43.6 us
    dot_general x6, matrix products, matmul(): return jnp.dot(left, right, preferred_element_type=F32)  31.3 us
    all_gather x1, waiting for transfers between devices, local(): layer_out = pick(lax.all_gather(out, 'rep', axis=0, tiled=True), sources)  26.5 us
    dot_general x6, matrix products, right_trans(): lax.dot_general(left, right, (((1,), (1,)), ((), ())), preferred_element_...  25.8 us
  transfers between devices with their start and end apart: 11, of which 11 were waited for; matrix products, arithmetic and copies ran while one was open for 10% of the time, Pallas kernels for 0%

profile of v1, /device:TPU:0, one launch (start us, length us, event | category | flops | bytes accessed | tf_op | source)
XLA Modules:
  0.0 909.0 jit_solution(15696778140888207360)
XLA Ops:
  8.0 2.2 pad_maximum_fusion.1
  18.1 10.6 %all-gather.3 = bf16[8,1,1536]{2,1,0:T(2,128)(2,1)S(1)} all-gather(bf16[1,1,1536]{2,1,0:T(2,128)(2,1)S(1)} %reshape.386), channel_id=1, replica_groups=mesh['shard'=8,'rep'=4] {'shard'}, dimensions={0}, use_global_device_ids=true | all-gather | bytes 27648 | tf_op jit(solution)/shard_map/all_gather | solution.py:108
  30.9 62.3 %all-gather.21.cloned.1.call-done = bf16[8,256,1024]{2,1,0:T(8,128)(2,1)} async-done(((bf16[2,256,1024]{2,1,0:T(8,128)(2,1)}), bf16[8,256,1024]{2,1,0:T(8,128)(2,1)}) %all-gather.21.cloned.1.call-update) | async-done | bytes 4194320 | tf_op jit(solution)/shard_map/all_gather | solution.py:129
  95.5 53.0 %all-gather.13.cloned.1.call-done = bf16[4096,1024]{1,0:T(8,128)(2,1)} async-done(((bf16[512,1024]{1,0:T(8,128)(2,1)}), bf16[4096,1024]{1,0:T(8,128)(2,1)}) %all-gather.13.cloned.1.call-update) | async-done | bytes 8388624 | tf_op jit(solution)/shard_map/all_gather | solution.py:101
  148.5 5.9 fusion.97
  154.4 1.3 copy-done.6
  157.4 4.7 fusion.43
  162.1 1.3 reshape.332
  163.4 4.5 fusion.53
  168.0 2.1 reshape.331
  170.1 2.5 fusion.59
  172.6 3.5 fusion.101
  177.0 3.3 copy-done.39
  182.1 1.4 fusion.102
  183.9 21.0 %all-gather.15.cloned.1.call-done = bf16[1024,4096]{1,0:T(8,128)(2,1)} async-done(((bf16[128,4096]{1,0:T(8,128)(2,1)}), bf16[1024,4096]{1,0:T(8,128)(2,1)}) %all-gather.15.cloned.1.call-update) | async-done | bytes 8388624 | tf_op jit(solution)/shard_map/all_gather | solution.py:101
  204.8 10.9 %multiply_convert_fusion.1 = (bf16[512,4096]{1,0:T(8,128)(2,1)}, f32[512,4096]{1,0:T(8,128)}) fusion(f32[4096]{0:T(1024)S(1)} %bitcast.247, bf16[1024,4096]{1,0:T(8,128)(2,1)} %all-gather.15.cloned.1.call-done, f32[512,1024]{1,0:T(8,128)S(1)} %get-tuple-element.66, f32[1024]{0:T(1024)S(1)} %get-tuple-element.54, f32[1024]{0:T(1024)S(1)} %get-tuple-element.55, ...), kind=kOutput, calls=%fused_computation.16 | convolution fusion | flops 4310171648 | bytes 23097344 | tf_op jit(solution)/shard_map/dot_general | solution.py:21
  215.8 45.2 %all-gather.17.cloned.1.call-done = bf16[4096,1024]{1,0:T(8,128)(2,1)} async-done(((bf16[512,1024]{1,0:T(8,128)(2,1)}), bf16[4096,1024]{1,0:T(8,128)(2,1)}) %all-gather.17.cloned.1.call-update) | async-done | bytes 8388624 | tf_op jit(solution)/shard_map/all_gather | solution.py:101
  261.0 8.5 fusion.103
  270.7 2.2 fusion.95
  273.0 12.0 %convert_reduce_fusion = (f32[4096]{0:T(1024)S(1)}, bf16[512,4096]{1,0:T(8,128)(2,1)S(1)}) fusion(f32[512,4096]{1,0:T(8,128)} %get-tuple-element.68, f32[4096]{0:T(1024)S(1)} %bitcast.248, bf16[4096,1024]{1,0:T(8,128)(2,1)} %all-gather.17.cloned.1.call-done, f32[512,1024]{1,0:T(8,128)S(1)} %get-tuple-element.27), kind=kOutput, calls=%fused_computation.12 | convolution fusion | flops 4322750464 | bytes 23101440 | tf_op jit(solution)/shard_map/dot_general | solution.py:29
  285.0 5.2 multiply_reduce_fusion.2
  292.2 2.3 convolution_convert_fusion.6
  294.5 2.4 copy.77
  296.9 2.1 reshape.336
  299.0 5.7 fusion.55
  304.7 13.5 %fusion.44 = bf16[2,256,16,64]{1,3,2,0:T(8,128)(2,1)} fusion(f32[2,16,256,256]{2,3,1,0:T(8,128)} %fusion.55, bf16[2,256,16,64]{1,0,3,2:T(2,128)(2,1)} %reshape.331, f32[2,16,256,256]{2,3,1,0:T(8,128)} %copy-done.39, f32[2,16,256]{2,1,0:T(8,128)S(1)} %get-tuple-element.63), kind=kOutput, calls=%fused_computation.72 | convolution fusion | flops 283648256 | bytes 18907136 | tf_op jit(solution)/shard_map/bhqk,bhqd->bhkd/dot_general | solution.py:195
  318.2 13.3 %convert_reduce_fusion.2 = (f32[16,64]{1,0:T(8,128)S(1)}, bf16[2,256,16,64]{1,3,2,0:T(8,128)(2,1)}) fusion(f32[2,16,256,256]{2,3,1,0:T(8,128)} %fusion.55, f32[2,16,256,256]{2,3,1,0:T(8,128)} %copy-done.39, f32[2,16,256]{2,1,0:T(8,128)S(1)} %get-tuple-element.63, bf16[2,256,16,64]{1,0,3,2:T(2,128)(2,1)S(1)} %copy-done.11), kind=kOutput, calls=%fused_computation.33 | convolution fusion | flops 284695808 | bytes 18911232 | tf_op jit(solution)/shard_map/bhqk,bhkd->bhqd/dot_general | solution.py:192
  331.5 5.2 convert_reduce_fusion.1
  346.3 3.7 pad_maximum_fusion
  350.1 9.8 %convolution_convert_fusion.1 = bf16[1024,4096]{1,0:T(8,128)(2,1)} fusion(bf16[512,4096]{1,0:T(8,128)(2,1)} %copy-done.40, f32[512,1024]{1,0:T(8,128)S(1)} %get-tuple-element.66, f32[1024]{0:T(1024)S(1)} %get-tuple-element.54, f32[1024]{0:T(1024)S(1)} %get-tuple-element.55, f32[512]{0:T(512)S(1)} %add_rsqrt_fusion.1, f32[512]{0:T(512)S(1)} %broadcast_multiply_fusion.4), kind=kOutput, calls=%fused_computation.21 | convolution fusion | flops 4301783040 | bytes 14692352 | tf_op jit(solution)/shard_map/dot_general | solution.py:25
  359.9 2.0 copy-done.17
  361.9 9.9 %convolution_convert_fusion = bf16[4096,1024]{1,0:T(8,128)(2,1)} fusion(bf16[512,4096]{1,0:T(8,128)(2,1)} %get-tuple-element.67, f32[512,1024]{1,0:T(8,128)S(1)} %copy-done.17), kind=kOutput, calls=%fused_computation.20 | convolution fusion | flops 4299685888 | bytes 14680064 | tf_op jit(solution)/shard_map/dot_general | solution.py:25
  372.6 48.8 %reduce-scatter.4.cloned.1.call-done = bf16[512,1024]{1,0:T(8,128)(2,1)} async-done(((bf16[4096,1024]{1,0:T(8,128)(2,1)}), bf16[512,1024]{1,0:T(8,128)(2,1)}) %reduce-scatter.4.cloned.1.call-update) | async-done | bytes 1048592 | tf_op jit(solution)/shard_map/reduce_scatter | solution.py:171
  421.5 74.9 %reduce-scatter.6.cloned.1.call-done = bf16[128,4096]{1,0:T(8,128)(2,1)} async-done(((bf16[1024,4096]{1,0:T(8,128)(2,1)}), bf16[128,4096]{1,0:T(8,128)(2,1)}) %reduce-scatter.6.cloned.1.call-update) | async-done | bytes 1048592 | tf_op jit(solution)/shard_map/reduce_scatter | solution.py:171
  496.5 74.7 %reduce-scatter.8.cloned.1.call-done = bf16[512,1024]{1,0:T(8,128)(2,1)} async-done(((bf16[4096,1024]{1,0:T(8,128)(2,1)}), bf16[512,1024]{1,0:T(8,128)(2,1)}) %reduce-scatter.8.cloned.1.call-update) | async-done | bytes 1048592 | tf_op jit(solution)/shard_map/reduce_scatter | solution.py:171
  575.9 43.6 %psum.7 = f32[8,1536]{1,0:T(8,128)S(1)} all-reduce(f32[8,1536]{1,0:T(8,128)S(1)} %constant_dynamic-update-slice_fusion), channel_id=1, replica_groups=mesh['shard'=8,'rep'=4] {'shard','rep'}, use_global_device_ids=true, to_apply=%region_23.25 | all-reduce | flops 12288 | bytes 98304 | tf_op jit(solution)/shard_map/psum | solution.py:233
  620.8 2.7 fusion.107
  625.8 2.3 add_convert_fusion
  628.1 26.5 %all-gather.19.cloned.1.call-done = bf16[8,256,1024]{2,1,0:T(8,128)(2,1)} async-done(((bf16[2,256,1024]{2,1,0:T(8,128)(2,1)}), bf16[8,256,1024]{2,1,0:T(8,128)(2,1)}) %all-gather.19.cloned.1.call-update) | async-done | bytes 4194320 | tf_op jit(solution)/shard_map/all_gather | solution.py:162
  656.9 78.6 %all-gather.23.cloned.1.call-done = bf16[2048,1024]{1,0:T(8,128)(2,1)} async-done(((bf16[512,1024]{1,0:T(8,128)(2,1)}), bf16[2048,1024]{1,0:T(8,128)(2,1)}) %all-gather.23.cloned.1.call-update) | async-done | bytes 4194320 | tf_op jit(solution)/shard_map/all_gather | solution.py:15
  735.6 3.3 reduce_sum.227
  738.9 77.5 %all-gather.25.cloned.1.call-done = bf16[512,4096]{1,0:T(8,128)(2,1)} async-done(((bf16[128,4096]{1,0:T(8,128)(2,1)}), bf16[512,4096]{1,0:T(8,128)(2,1)}) %all-gather.25.cloned.1.call-update) | async-done | bytes 4194320 | tf_op jit(solution)/shard_map/all_gather | solution.py:15
  816.4 3.1 reduce_sum.237
  819.4 1.5 convert_element_type.290
  821.0 1.4 fusion.98
  822.4 75.0 %all-gather.27.cloned.1.call-done = bf16[2048,1024]{1,0:T(8,128)(2,1)} async-done(((bf16[512,1024]{1,0:T(8,128)(2,1)}), bf16[2048,1024]{1,0:T(8,128)(2,1)}) %all-gather.27.cloned.1.call-update) | async-done | bytes 4194320 | tf_op jit(solution)/shard_map/all_gather | solution.py:15
  897.4 3.3 reduce_sum.238
  900.7 1.6 convert_element_type.292
  (180 shorter events, 33.9 us)
Async XLA Ops:
  7.2 21.6 %copy-start = (s32[64]{0:T(128)S(1)}, s32[64]{0:T(128)}, u32[]{:S(2)}) copy-start(s32[64]{0:T(128)} %param.22) | copy-start | bytes 772
  7.2 86.0 %all-gather.21.cloned.1.call-start = ((), (), s32[]{:S(2)}) async-start(), calls=%async_computation.7 | async-start | bytes 5242880 | tf_op jit(solution)/shard_map/all_gather | solution.py:129
  7.9 140.6 %all-gather.13.cloned.1.call-start = ((), (), s32[]{:S(2)}) async-start(), calls=%async_computation.3 | async-start | bytes 9437184 | tf_op jit(solution)/shard_map/all_gather | solution.py:101
  10.2 6.1 copy-start.31
  10.2 6.4 copy-start.32
  10.2 6.6 copy-start.33
  10.2 6.8 copy-start.34
  10.2 7.0 copy-start.35
  10.3 7.2 copy-start.36
  10.3 7.4 copy-start.37
  10.3 7.6 copy-start.38
  10.3 7.8 copy-start.30
  10.3 194.5 %all-gather.15.cloned.1.call-start = ((), (), s32[]{:S(2)}) async-start(), calls=%async_computation.4 | async-start | bytes 9437184 | tf_op jit(solution)/shard_map/all_gather | solution.py:101
  11.1 249.9 %all-gather.17.cloned.1.call-start = ((), (), s32[]{:S(2)}) async-start(), calls=%async_computation.5 | async-start | bytes 9437184 | tf_op jit(solution)/shard_map/all_gather | solution.py:101
  11.6 409.8 %reduce-scatter.4.cloned.1.call-start = ((), (), s32[]{:S(2)}) async-start(), calls=%async_computation.8 | async-start | bytes 9437184 | tf_op jit(solution)/shard_map/reduce_scatter | solution.py:171
  148.5 7.2 copy-start.25
  157.4 18.8 %copy-start.12 = (bf16[2,256,16,64]{1,0,3,2:T(2,128)(2,1)}, bf16[2,256,16,64]{1,0,3,2:T(2,128)(2,1)S(1)}, u32[]{:S(2)}) copy-start(bf16[2,256,16,64]{1,0,3,2:T(2,128)(2,1)S(1)} %reshape.333) | copy-start | bytes 3145732
  163.4 6.7 copy-start.10
  176.1 4.2 copy-start.39
  180.3 1.9 copy-start.26
  181.6 1.9 copy-start.14
  270.7 14.2 %slice-start = ((s8[8388608]{0:T(1024)(128)(4,1)}), s8[4194304]{0:T(1024)(128)(4,1)S(1)}, s32[]{:S(2)}) async-start(s8[8388608]{0:T(1024)(128)(4,1)} %bitcast.251), calls=%async_computation.14 | async-start | bytes 8388608
  273.0 12.0 %copy-start.16 = (f32[512,1024]{1,0:T(8,128)}, f32[512,1024]{1,0:T(8,128)S(1)}, u32[]{:S(2)}) copy-start(f32[512,1024]{1,0:T(8,128)S(1)} %get-tuple-element.27) | copy-start | bytes 6291460
  273.0 12.0 %slice-start.1 = ((s8[8388608]{0:T(1024)(128)(4,1)}), s8[4194304]{0:T(1024)(128)(4,1)S(1)}, s32[]{:S(2)}) async-start(s8[8388608]{0:T(1024)(128)(4,1)} %bitcast.251), calls=%async_computation.15 | async-start | bytes 8388608
  284.9 5.3 copy-start.40
  290.2 2.0 copy-start.9
  294.5 4.5 copy-start.13
  304.7 13.5 %copy-start.11 = (bf16[2,256,16,64]{1,0,3,2:T(2,128)(2,1)S(1)}, bf16[2,256,16,64]{1,0,3,2:T(2,128)(2,1)}, u32[]{:S(2)}) copy-start(bf16[2,256,16,64]{1,0,3,2:T(2,128)(2,1)} %copy-done.10) | copy-start | bytes 3145732
  331.5 5.3 copy-start.4
  331.5 5.3 copy-start.15
  339.4 4.3 copy-start.20
  340.8 4.2 copy-start.21
  340.8 1.6 copy-start.27
  350.0 146.4 %reduce-scatter.6.cloned.1.call-start = ((), (), s32[]{:S(2)}) async-start(), calls=%async_computation.9 | async-start | bytes 9437184 | tf_op jit(solution)/shard_map/reduce_scatter | solution.py:171
  359.9 2.0 copy-start.17
  359.9 211.3 %reduce-scatter.8.cloned.1.call-start = ((), (), s32[]{:S(2)}) async-start(), calls=%async_computation.10 | async-start | bytes 9437184 | tf_op jit(solution)/shard_map/reduce_scatter | solution.py:171
  371.8 282.8 %all-gather.19.cloned.1.call-start = ((), (), s32[]{:S(2)}) async-start(), calls=%async_computation.6 | async-start | bytes 5242880 | tf_op jit(solution)/shard_map/all_gather | solution.py:162
  371.8 199.3 %copy-start.29 = (s32[2]{0:T(128)S(1)}, s32[2]{0:T(128)}, u32[]{:S(2)}) copy-start(s32[2]{0:T(128)} %get-tuple-element.78) | copy-start | bytes 28
  371.9 204.0 %copy-start.28 = (f32[1024]{0:T(1024)S(1)}, f32[1024]{0:T(1024)}, u32[]{:S(2)}) copy-start(f32[1024]{0:T(1024)} %get-tuple-element.24) | copy-start | bytes 12292
  371.9 248.9 %copy-start.19 = (bf16[8,1,128,1024]{3,2,1,0:T(8,128)(2,1)S(1)}, bf16[8,1,128,1024]{3,2,1,0:T(8,128)(2,1)}, u32[]{:S(2)}) copy-start(bf16[8,1,128,1024]{3,2,1,0:T(8,128)(2,1)} %get-tuple-element.32) | copy-start | bytes 6291460
  372.5 363.0 %all-gather.23.cloned.1.call-start = ((), (), s32[]{:S(2)}) async-start(), calls=%async_computation.11 | async-start | bytes 5242880 | tf_op jit(solution)/shard_map/all_gather | solution.py:15
  421.4 394.9 %all-gather.25.cloned.1.call-start = ((), (), s32[]{:S(2)}) async-start(), calls=%async_computation.12 | async-start | bytes 5242880 | tf_op jit(solution)/shard_map/all_gather | solution.py:15
  496.4 400.9 %all-gather.27.cloned.1.call-start = ((), (), s32[]{:S(2)}) async-start(), calls=%async_computation.13 | async-start | bytes 5242880 | tf_op jit(solution)/shard_map/all_gather | solution.py:15
  620.8 2.7 copy-start.18
  620.8 2.8 copy-start.22
  623.5 1.6 copy-start.5
  623.6 2.2 copy-start.7
  897.4 4.9 copy-start.1
  (6 other events, 8.4 us)
Sparse Core Ops, SparseCore 0:
  9.6 83.5 all-gather.20
  95.6 52.8 all-gather.12
  150.4 54.3 all-gather.14
  206.6 54.3 all-gather.16
  350.1 71.2 reduce-scatter.3
  425.1 71.2 reduce-scatter.5
  499.9 71.2 reduce-scatter.7
  572.8 81.7 all-gather.18
  656.2 79.2 all-gather.22
  737.0 79.2 all-gather.24
  818.0 79.2 all-gather.26
